TPU v7x, 128 devices: a whole 4x4x4 slice. The times are simulated.
128 devices in a mesh: src: 4 (over z_hi, core), rcv: 32 (over y, z_lo, x).
Axes of the slice: x: 4, y: 4, z: 4 (z_hi: 2, z_lo: 2; z = z_hi * 2 + z_lo), core: 2. Of those that a mesh axis runs over, the one named last changes fastest.
Arguments:
- traces: bfloat16 [4096, 16, 2000], P('rcv', 'src')
- src_index: int32 [256], P('src'), may hold values from 0 to 4095, as said below
- quality: int32 [4096, 16], P('rcv'), may hold values 0 or 1
Outputs:
- xcorr: float32 [256, 201, 4096], P('src', None, 'rcv')
Inputs may be any that keep to these rules, and one draw needn't show every extreme that they name: `src_index`: the source numbered j within each group of 64 sources lies in receiver block j mod 32, among channels (j mod 32) * 128 up to that plus 128 - 1.
All inputs are finite; a program needn't handle non-finite values. No bound on the sum of `quality` on one device may be relied on, other than what follows from the above.
Results may differ from a plain program's by a relative error of at most 0.0067.
Values may be sent and summed in bfloat16 or wider, within the bound.
No kernel may reach another device: no remote copies, remote signals or barrier semaphores. Data moves between devices by JAX's collectives and lax.ppermute only.
A program may use at most 576 MiB of HBM per device.

v0:
```python
import math
import jax
import jax.numpy as jnp
from jax import lax
from jax.sharding import PartitionSpec as P

LAGH = 100


def make_tables(length):
    half = length // 2
    bins = jnp.arange(1, half + 1, dtype=jnp.int32)
    times = jnp.arange(length, dtype=jnp.int32)
    phase = (times[:, None] * bins[None, :] % length).astype(jnp.float32) * (2.0 * math.pi / length)
    forward = jnp.concatenate([jnp.cos(phase), -jnp.sin(phase)], axis=1).astype(jnp.bfloat16)
    lagvals = jnp.arange(-LAGH, LAGH + 1, dtype=jnp.int32)
    phase_lag = (bins[:, None] * lagvals[None, :] % length).astype(jnp.float32) * (
        2.0 * math.pi / length
    )
    weights = jnp.where(bins == half, 1.0, 2.0).astype(jnp.float32)[:, None] / jnp.sqrt(
        jnp.float32(half)
    )
    inverse = jnp.concatenate(
        [weights * jnp.cos(phase_lag), -weights * jnp.sin(phase_lag)], axis=0
    ).astype(jnp.bfloat16)
    return (forward, inverse)


def whiten(samples, forward):
    length = samples.shape[2]
    half = length // 2
    spec = jnp.dot(samples.reshape(-1, length), forward, preferred_element_type=jnp.float32)
    real_part = spec[:, :half]
    imag_part = spec[:, half:]
    power = real_part * real_part + imag_part * imag_part
    level = 0.5 * jnp.sqrt(jnp.mean(power, axis=1, keepdims=True) + 1e-06)
    denom = jnp.maximum(jnp.sqrt(power), level)
    white = jnp.concatenate([real_part / denom, imag_part / denom], axis=1).astype(jnp.bfloat16)
    return white.reshape(samples.shape[0], samples.shape[1], length)


def on_device(traces, src_index, quality):
    rows, seg_local, length = traces.shape
    half = length // 2
    nsrc = src_index.shape[0]
    seg_all = quality.shape[1]
    forward, inverse = make_tables(length)
    white_local = whiten(traces, forward)
    white_all = lax.all_gather(white_local, "src", axis=1, tiled=True)
    qual = quality.astype(jnp.bfloat16)
    first_channel = lax.axis_index("rcv") * rows
    onehot = (
        src_index[:, None] == first_channel + jnp.arange(rows, dtype=jnp.int32)[None, :]
    ).astype(jnp.bfloat16)
    found = jnp.dot(onehot, white_all.reshape(rows, -1), preferred_element_type=jnp.float32)
    flags = jnp.dot(onehot, qual, preferred_element_type=jnp.float32)
    found, flags = (
        lax.psum(found.astype(jnp.bfloat16), "rcv").astype(jnp.float32),
        lax.psum(flags.astype(jnp.bfloat16), "rcv").astype(jnp.float32),
    )
    srcw = found.reshape(nsrc, seg_all, length).astype(jnp.bfloat16)
    msrc = flags.astype(jnp.bfloat16)
    count = jnp.dot(msrc, qual.T, preferred_element_type=jnp.float32)
    recv = white_all * qual[:, :, None]
    recv_re = recv[:, :, :half]
    recv_im = recv[:, :, half:]
    left_all = srcw * msrc[:, :, None]
    group = 8
    left_blocks = left_all.reshape(nsrc // group, group, seg_all, length)

    def one_block(left):
        left_re = left[:, :, :half]
        left_im = left[:, :, half:]
        pre = jnp.einsum("isk,jsk->ijk", left_re, recv_re, preferred_element_type=jnp.float32)
        pre = pre + jnp.einsum("isk,jsk->ijk", left_im, recv_im, preferred_element_type=jnp.float32)
        pim = jnp.einsum("isk,jsk->ijk", left_im, recv_re, preferred_element_type=jnp.float32)
        pim = pim - jnp.einsum("isk,jsk->ijk", left_re, recv_im, preferred_element_type=jnp.float32)
        cross = jnp.concatenate([pre, pim], axis=2).astype(jnp.bfloat16)
        return jnp.einsum("ijk,kt->itj", cross, inverse, preferred_element_type=jnp.float32)

    lagged = lax.map(one_block, left_blocks)
    lagged = lagged.reshape(nsrc, 2 * LAGH + 1, rows)
    return lagged / jnp.maximum(count, 1.0)[:, None, :]


def solution(mesh):
    return jax.shard_map(
        on_device,
        mesh=mesh,
        in_specs=(P("rcv", "src", None), P("src"), P("rcv", None)),
        out_specs=P("src", None, "rcv"),
        check_vma=False,
    )
```

profile of v0, /device:TPU:1, one launch (start us, length us, event | category | flops | bytes accessed | tf_op | source)
XLA Modules:
  0.0 1214.9 jit_solution(14916867752042446205)
XLA Ops:
  6.5 35.3 %cosine_convert_fusion = (bf16[2000,1000]{1,0:T(8,128)(2,1)}, bf16[2000,1000]{1,0:T(8,128)(2,1)}) fusion(s32[1000]{0:T(1024)S(1)} %iota_add_fusion), kind=kLoop, calls=%fused_computation.36 | loop fusion | flops 24000000 | bytes 8004000 | tf_op jit(solution)/shard_map/convert.10
  41.9 3.4 copy.17
  47.6 10.1 fusion.37
  62.0 2.8 pad_maximum_fusion.1
  64.8 3.0 copy.20
  67.9 65.1 %all-gather.2.cloned.1.call-done = bf16[128,16,2000]{0,2,1:T(8,128)(2,1)} async-done(((bf16[128,4,2000]{0,2,1:T(8,128)(2,1)}), bf16[128,16,2000]{0,2,1:T(8,128)(2,1)}) %all-gather.2.cloned.1.call-update) | async-done | bytes 8192016 | tf_op jit(solution)/shard_map/all_gather | solution.py:49
  133.0 8.3 convolution_convert_fusion
  141.2 9.6 convert_element_type.35
  150.9 31.0 %copy.21 = bf16[8,8,16,2000]{2,1,3,0:T(8,128)(2,1)} copy(bf16[8,8,16,2000]{3,2,1,0:T(8,128)(2,1)} %convert_element_type.35) | data formatting | bytes 8192000 | tf_op jit(solution)/shard_map/convert_element_type | solution.py:61
  182.8 76.6 %psum.15 = bf16[64,16]{0,1:T(8,128)(2,1)S(1)} all-reduce(bf16[64,16]{0,1:T(8,128)(2,1)S(1)} %convolution_convert_fusion.1), channel_id=1, replica_groups=mesh['src'=4,'rcv'=32] {'rcv'}, use_global_device_ids=true, to_apply=%region_2.3 | all-reduce | flops 1024 | bytes 4096 | tf_op jit(solution)/shard_map/psum | solution.py:59
  260.3 3.7 multiply_convert_fusion.1
  265.2 7.3 broadcast_multiply_fusion.1
  272.5 3.8 fusion.54
  276.3 2.5 copy.23
  281.3 611.0 %all-reduce.2.cloned.1.call-done = bf16[8,8,16,2000]{2,1,3,0:T(8,128)(2,1)} async-done(((bf16[8,8,16,2000]{2,1,3,0:T(8,128)(2,1)}), bf16[8,8,16,2000]{2,1,3,0:T(8,128)(2,1)}) %all-reduce.2.cloned.1.call-update) | async-done | bytes 4096016 | tf_op jit(solution)/shard_map/psum | solution.py:58
  892.3 22.5 %broadcast_multiply_fusion = bf16[8,8,16,2000]{2,1,3,0:T(8,128)(2,1)} fusion(bf16[8,8,16,2000]{2,1,3,0:T(8,128)(2,1)} %all-reduce.2.cloned.1.call-done, bf16[8,8,16]{2,1,0:T(8,128)(2,1)S(1)} %bitcast.91), kind=kLoop, calls=%fused_computation.27 | loop fusion | flops 2048000 | bytes 8194048 | tf_op jit(solution)/shard_map/mul | solution.py:67
  914.8 285.8 %while.10 = (s32[]{:T(128)}, f32[8,8,201,128]{3,1,0,2:T(8,128)}, bf16[8,8,16,2000]{2,1,3,0:T(8,128)(2,1)}, bf16[128,16,1000]{0,1,2:T(8,128)(2,1)}, bf16[128,16,1...) while((s32[]{:T(128)}, f32[8,8,201,128]{3,1,0,2:T(8,128)}, ...), condition=%wide.region_4.5_spmd, body=%wide.region_3.4_spmd.sunk | while | flops 960512000 | bytes 119130632 | solution.py:81
  915.0 2.5 fusion.110
  919.6 2.5 fusion.112
  923.0 2.5 fusion.113
  929.2 2.5 fusion.116
  934.2 14.2 %pad_maximum_fusion.4 = bf16[8,128,2000]{1,0,2:T(8,128)(2,1)S(1)} fusion(bf16[8,128,1000]{1,0,2:T(8,128)(2,1)S(1)} %copy-done, bf16[8,128,1000]{1,0,2:T(8,128)(2,1)S(1)} %fusion.117), kind=kLoop, calls=%fused_computation.clone.1 | loop fusion | flops 2048000 | bytes 8192000 | tf_op jit(solution)/shard_map/while/body/eval_jaxpr/concatenate | solution.py:78
  955.3 2.5 fusion.112
  958.7 2.5 fusion.113
  964.9 2.5 fusion.116
  969.9 14.2 %pad_maximum_fusion.4 = bf16[8,128,2000]{1,0,2:T(8,128)(2,1)S(1)} fusion(bf16[8,128,1000]{1,0,2:T(8,128)(2,1)S(1)} %copy-done, bf16[8,128,1000]{1,0,2:T(8,128)(2,1)S(1)} %fusion.117), kind=kLoop, calls=%fused_computation.clone.1 | loop fusion | flops 2048000 | bytes 8192000 | tf_op jit(solution)/shard_map/while/body/eval_jaxpr/concatenate | solution.py:78
  991.0 2.5 fusion.112
  994.4 2.5 fusion.113
  1000.6 2.5 fusion.116
  1005.5 14.2 %pad_maximum_fusion.4 = bf16[8,128,2000]{1,0,2:T(8,128)(2,1)S(1)} fusion(bf16[8,128,1000]{1,0,2:T(8,128)(2,1)S(1)} %copy-done, bf16[8,128,1000]{1,0,2:T(8,128)(2,1)S(1)} %fusion.117), kind=kLoop, calls=%fused_computation.clone.1 | loop fusion | flops 2048000 | bytes 8192000 | tf_op jit(solution)/shard_map/while/body/eval_jaxpr/concatenate | solution.py:78
  1026.7 2.5 fusion.112
  1030.1 2.5 fusion.113
  1036.3 2.5 fusion.116
  1041.3 14.2 %pad_maximum_fusion.4 = bf16[8,128,2000]{1,0,2:T(8,128)(2,1)S(1)} fusion(bf16[8,128,1000]{1,0,2:T(8,128)(2,1)S(1)} %copy-done, bf16[8,128,1000]{1,0,2:T(8,128)(2,1)S(1)} %fusion.117), kind=kLoop, calls=%fused_computation.clone.1 | loop fusion | flops 2048000 | bytes 8192000 | tf_op jit(solution)/shard_map/while/body/eval_jaxpr/concatenate | solution.py:78
  1062.4 2.5 fusion.112
  1065.8 2.5 fusion.113
  1072.0 2.5 fusion.116
  1077.0 14.2 %pad_maximum_fusion.4 = bf16[8,128,2000]{1,0,2:T(8,128)(2,1)S(1)} fusion(bf16[8,128,1000]{1,0,2:T(8,128)(2,1)S(1)} %copy-done, bf16[8,128,1000]{1,0,2:T(8,128)(2,1)S(1)} %fusion.117), kind=kLoop, calls=%fused_computation.clone.1 | loop fusion | flops 2048000 | bytes 8192000 | tf_op jit(solution)/shard_map/while/body/eval_jaxpr/concatenate | solution.py:78
  1098.1 2.5 fusion.112
  1101.5 2.5 fusion.113
  1107.7 2.5 fusion.116
  1112.7 14.2 %pad_maximum_fusion.4 = bf16[8,128,2000]{1,0,2:T(8,128)(2,1)S(1)} fusion(bf16[8,128,1000]{1,0,2:T(8,128)(2,1)S(1)} %copy-done, bf16[8,128,1000]{1,0,2:T(8,128)(2,1)S(1)} %fusion.117), kind=kLoop, calls=%fused_computation.clone.1 | loop fusion | flops 2048000 | bytes 8192000 | tf_op jit(solution)/shard_map/while/body/eval_jaxpr/concatenate | solution.py:78
  1137.2 2.5 fusion.113
  1143.4 2.5 fusion.116
  1148.4 14.2 %pad_maximum_fusion.4 = bf16[8,128,2000]{1,0,2:T(8,128)(2,1)S(1)} fusion(bf16[8,128,1000]{1,0,2:T(8,128)(2,1)S(1)} %copy-done, bf16[8,128,1000]{1,0,2:T(8,128)(2,1)S(1)} %fusion.117), kind=kLoop, calls=%fused_computation.clone.1 | loop fusion | flops 2048000 | bytes 8192000 | tf_op jit(solution)/shard_map/while/body/eval_jaxpr/concatenate | solution.py:78
  1172.9 2.5 fusion.113
  1184.0 14.2 %pad_maximum_fusion.4 = bf16[8,128,2000]{1,0,2:T(8,128)(2,1)S(1)} fusion(bf16[8,128,1000]{1,0,2:T(8,128)(2,1)S(1)} %copy-done, bf16[8,128,1000]{1,0,2:T(8,128)(2,1)S(1)} %fusion.117), kind=kLoop, calls=%fused_computation.clone.1 | loop fusion | flops 2048000 | bytes 8192000 | tf_op jit(solution)/shard_map/while/body/eval_jaxpr/concatenate | solution.py:78
  1200.6 7.2 bitcast_divide_fusion
  (167 shorter events, 127.4 us)
Async XLA Ops:
  6.5 126.4 %all-gather.2.cloned.1.call-start = ((), (), s32[]{:S(2)}) async-start(), calls=%async_computation | async-start | bytes 10240000 | tf_op jit(solution)/shard_map/all_gather | solution.py:49
  64.8 68.2 %copy-start.7 = (s32[64]{0:T(128)S(1)}, s32[64]{0:T(128)}, u32[]{:S(2)}) copy-start(s32[64]{0:T(128)} %param.6) | copy-start | bytes 772
  67.8 824.5 %all-reduce.2.cloned.1.call-start = ((), (), s32[]{:S(2)}) async-start(), calls=%async_computation.1 | async-start | bytes 65536000 | tf_op jit(solution)/shard_map/psum | solution.py:58
  181.9 0.7 copy-start.6
  914.8 285.8 %copy-start.5 = (f32[64,128]{1,0:T(8,128)S(1)}, f32[64,128]{1,0:T(8,128)}, u32[]{:S(2)}) copy-start(f32[64,128]{1,0:T(8,128)} %convolution_maximum_fusion) | copy-start | bytes 98308
  915.0 3.4 copy-start.1
  919.6 3.4 copy-start.3
  929.2 3.4 copy-start.2
  932.6 1.6 copy-start
  934.2 14.3 %copy-start.4 = (bf16[2000,201]{0,1:T(8,128)(2,1)S(1)}, bf16[2000,201]{0,1:T(8,128)(2,1)}, u32[]{:S(2)}) copy-start(bf16[2000,201]{0,1:T(8,128)(2,1)} %get-tuple-element.122) | copy-start | bytes 2412004 | tf_op jit(solution)/shard_map/while
  950.7 3.4 copy-start.1
  955.3 3.4 copy-start.3
  964.9 3.4 copy-start.2
  968.3 1.6 copy-start
  969.9 14.3 %copy-start.4 = (bf16[2000,201]{0,1:T(8,128)(2,1)S(1)}, bf16[2000,201]{0,1:T(8,128)(2,1)}, u32[]{:S(2)}) copy-start(bf16[2000,201]{0,1:T(8,128)(2,1)} %get-tuple-element.122) | copy-start | bytes 2412004 | tf_op jit(solution)/shard_map/while
  986.4 3.4 copy-start.1
  991.0 3.4 copy-start.3
  1000.6 3.4 copy-start.2
  1004.0 1.6 copy-start
  1005.5 14.3 %copy-start.4 = (bf16[2000,201]{0,1:T(8,128)(2,1)S(1)}, bf16[2000,201]{0,1:T(8,128)(2,1)}, u32[]{:S(2)}) copy-start(bf16[2000,201]{0,1:T(8,128)(2,1)} %get-tuple-element.122) | copy-start | bytes 2412004 | tf_op jit(solution)/shard_map/while
  1022.1 3.4 copy-start.1
  1026.7 3.4 copy-start.3
  1036.3 3.4 copy-start.2
  1039.7 1.6 copy-start
  1041.3 14.3 %copy-start.4 = (bf16[2000,201]{0,1:T(8,128)(2,1)S(1)}, bf16[2000,201]{0,1:T(8,128)(2,1)}, u32[]{:S(2)}) copy-start(bf16[2000,201]{0,1:T(8,128)(2,1)} %get-tuple-element.122) | copy-start | bytes 2412004 | tf_op jit(solution)/shard_map/while
  1057.8 3.4 copy-start.1
  1062.4 3.4 copy-start.3
  1072.0 3.4 copy-start.2
  1075.4 1.6 copy-start
  1077.0 14.3 %copy-start.4 = (bf16[2000,201]{0,1:T(8,128)(2,1)S(1)}, bf16[2000,201]{0,1:T(8,128)(2,1)}, u32[]{:S(2)}) copy-start(bf16[2000,201]{0,1:T(8,128)(2,1)} %get-tuple-element.122) | copy-start | bytes 2412004 | tf_op jit(solution)/shard_map/while
  1093.5 3.4 copy-start.1
  1098.1 3.4 copy-start.3
  1107.7 3.4 copy-start.2
  1111.1 1.6 copy-start
  1112.7 14.3 %copy-start.4 = (bf16[2000,201]{0,1:T(8,128)(2,1)S(1)}, bf16[2000,201]{0,1:T(8,128)(2,1)}, u32[]{:S(2)}) copy-start(bf16[2000,201]{0,1:T(8,128)(2,1)} %get-tuple-element.122) | copy-start | bytes 2412004 | tf_op jit(solution)/shard_map/while
  1129.2 3.4 copy-start.1
  1133.8 3.4 copy-start.3
  1143.4 3.4 copy-start.2
  1146.8 1.6 copy-start
  1148.4 14.3 %copy-start.4 = (bf16[2000,201]{0,1:T(8,128)(2,1)S(1)}, bf16[2000,201]{0,1:T(8,128)(2,1)}, u32[]{:S(2)}) copy-start(bf16[2000,201]{0,1:T(8,128)(2,1)} %get-tuple-element.122) | copy-start | bytes 2412004 | tf_op jit(solution)/shard_map/while
  1164.9 3.4 copy-start.1
  1169.5 3.4 copy-start.3
  1179.1 3.4 copy-start.2
  1182.5 1.6 copy-start
  1184.0 14.3 %copy-start.4 = (bf16[2000,201]{0,1:T(8,128)(2,1)S(1)}, bf16[2000,201]{0,1:T(8,128)(2,1)}, u32[]{:S(2)}) copy-start(bf16[2000,201]{0,1:T(8,128)(2,1)} %get-tuple-element.122) | copy-start | bytes 2412004 | tf_op jit(solution)/shard_map/while
Sparse Core Ops, SparseCore 0:
  67.9 64.9 all-gather.1
  182.0 710.2 all-reduce.1
where the time goes:
time: 1220 us; the launch traced here: 1210 us
  waiting for transfers between devices  676 us (55%)
  other arithmetic  195 us (16%)
  local copies, waits for them, and re-layouts  174 us (14%)
  matrix products  77.6 us (6%)
  blocking collectives  76.6 us (6%)
  between operations  13.9 us (1%)
    psum x1, waiting for transfers between devices, on_device(): lax.psum(found.astype(jnp.bfloat16), 'rcv').astype(jnp.float32)  611 us
    concatenate x8, other arithmetic, one_block(): cross = jnp.concatenate([pre, pim], axis=2).astype(jnp.bfloat16)  114 us
    psum x1, blocking collectives, on_device(): lax.psum(flags.astype(jnp.bfloat16), 'rcv').astype(jnp.float32)  76.6 us
    all_gather x1, waiting for transfers between devices, on_device(): white_all = lax.all_gather(white_local, 'src', axis=1, tiled=True)  65.1 us
    convert_element_type x2, local copies, waits for them, and re-layouts, on_device(): srcw = found.reshape(nsrc, seg_all, length).astype(jnp.bfloat16)  40.6 us
    another operation x3, other arithmetic  40 us
  transfers between devices with their start and end apart: 2, of which 2 were waited for; matrix products, arithmetic and copies ran while one was open for 2% of the time, Pallas kernels for 0%

commit v1 on v0

--- a/solution.py
+++ b/solution.py
@@ -5,6 +5,13 @@
 from jax.sharding import PartitionSpec as P
 
 LAGH = 100
+
+
+def exchange_gather(x, axis, d):
+    count = lax.axis_size(axis)
+    blocks = jnp.stack([x for _ in range(count)])
+    blocks = lax.all_to_all(blocks, axis, split_axis=0, concat_axis=0)
+    return jnp.concatenate(blocks, axis=d)
 
 
 def make_tables(length):
@@ -46,7 +53,7 @@
     seg_all = quality.shape[1]
     forward, inverse = make_tables(length)
     white_local = whiten(traces, forward)
-    white_all = lax.all_gather(white_local, "src", axis=1, tiled=True)
+    white_all = exchange_gather(white_local, "src", 1)
     qual = quality.astype(jnp.bfloat16)
     first_channel = lax.axis_index("rcv") * rows
     onehot = (

time: 1220 us -> 876 us (0.72)
  the two profiles are of different devices: /device:TPU:1 before, /device:TPU:0 now
where the time goes in v1:
time: 876 us; the launch traced here: 873 us
  waiting for transfers between devices  298 us (34%)
  local copies, waits for them, and re-layouts  224 us (26%)
  matrix products  129 us (15%)
  other arithmetic  119 us (14%)
  blocking collectives  83.5 us (10%)
  between operations  13.5 us (2%)
    psum x1, waiting for transfers between devices, on_device(): lax.psum(found.astype(jnp.bfloat16), 'rcv').astype(jnp.float32)  206 us
    another operation x18, local copies, waits for them, and re-layouts  118 us
    all_to_all x1, waiting for transfers between devices, exchange_gather(): blocks = lax.all_to_all(blocks, axis, split_axis=0, concat_axis=0)  92.6 us
    psum x1, blocking collectives, on_device(): lax.psum(flags.astype(jnp.bfloat16), 'rcv').astype(jnp.float32)  83.5 us
    add x8, other arithmetic, one_block(): pre + jnp.einsum('isk,jsk->ijk', left_im, recv_im, preferred_element_type...  57.7 us
    another operation x3, other arithmetic  39 us
    dot_general x8, matrix products, one_block(): jnp.einsum('isk,jsk->ijk', left_im, recv_re, preferred_element_type=jnp.f...  28 us
    dot_general x8, matrix products, one_block(): jnp.einsum('isk,jsk->ijk', left_re, recv_re, preferred_element_type=jnp.f...  25.9 us
  transfers between devices with their start and end apart: 2, of which 2 were waited for; matrix products, arithmetic and copies ran while one was open for 4% of the time, Pallas kernels for 0%

profile of v1, /device:TPU:0, one launch (start us, length us, event | category | flops | bytes accessed | tf_op | source)
XLA Modules:
  0.0 872.8 jit_solution(7205208822910881751)
XLA Ops:
  12.3 34.3 %cosine_convert_fusion = (bf16[2000,1000]{1,0:T(8,128)(2,1)S(1)}, bf16[2000,1000]{1,0:T(8,128)(2,1)S(1)}) fusion(s32[1000]{0:T(1024)S(1)} %iota_add_fusion), kind=kLoop, calls=%fused_computation.25 | loop fusion | flops 24000000 | bytes 8004000 | tf_op jit(solution)/shard_map/convert.10
  46.6 6.1 fusion.22
  62.6 5.9 stack.3
  68.4 5.8 all-to-all-start
  74.3 92.6 %all-to-all-done = bf16[4,128,4,2000]{1,3,2,0:T(8,128)(2,1)} async-done(((bf16[4,128,4,2000]{1,3,2,0:T(8,128)(2,1)}), bf16[4,128,4,2000]{1,3,2,0:T(8,128)(2,1)}, u32[]{:S(2)}, u32[]{:S(2)}) %all-to-all-start) | async-done | bytes 8192032 | tf_op jit(solution)/shard_map/all_to_all | solution.py:13
  166.9 8.3 convolution_convert_fusion
  175.2 9.6 %convert_element_type.36 = bf16[8,8,16,2000]{3,2,1,0:T(8,128)(2,1)} reshape(bf16[64,32000]{1,0:T(8,128)(2,1)} %convolution_convert_fusion) | data formatting | bytes 8192000 | tf_op jit(solution)/shard_map/convert_element_type | solution.py:68
  185.7 83.5 %psum.15 = bf16[64,16]{0,1:T(8,128)(2,1)S(1)} all-reduce(bf16[64,16]{0,1:T(8,128)(2,1)S(1)} %convolution_convert_fusion.1), channel_id=1, replica_groups=mesh['src'=4,'rcv'=32] {'rcv'}, use_global_device_ids=true, to_apply=%region_2.3 | all-reduce | flops 1024 | bytes 4096 | tf_op jit(solution)/shard_map/psum | solution.py:66
  270.1 3.7 multiply_convert_fusion.1
  274.1 7.2 bitcast_multiply_fusion
  281.2 5.7 fusion.40
  287.0 6.9 copy.14
  293.8 6.8 copy.13
  300.6 205.9 %all-reduce.2.cloned.1.call-done = bf16[8,8,16,2000]{3,2,1,0:T(8,128)(2,1)} async-done(((bf16[8,8,16,2000]{3,2,1,0:T(8,128)(2,1)}), bf16[8,8,16,2000]{3,2,1,0:T(8,128)(2,1)}) %all-reduce.2.cloned.1.call-update) | async-done | bytes 4096016 | tf_op jit(solution)/shard_map/psum | solution.py:65
  506.5 4.5 broadcast_multiply_fusion
  511.1 347.8 %while.10 = (s32[]{:T(128)}, f32[8,8,201,128]{3,1,0,2:T(8,128)}, bf16[8,8,16,2000]{3,2,1,0:T(8,128)(2,1)}, bf16[128,16,1000]{2,1,0:T(8,128)(2,1)}, bf16[128,16,1...) while((s32[]{:T(128)}, f32[8,8,201,128]{3,1,0,2:T(8,128)}, ...), condition=%wide.region_4.5_spmd, body=%wide.region_3.4_spmd.sunk | while | flops 966656000 | bytes 114890064 | solution.py:88
  516.8 7.3 copy.55
  524.1 7.3 copy.57
  531.4 3.5 fusion.89
  545.0 7.2 fusion.90
  560.3 7.3 copy.55
  567.6 7.3 copy.57
  574.9 3.5 fusion.89
  588.5 7.2 fusion.90
  603.8 7.3 copy.55
  611.0 7.3 copy.57
  618.3 3.5 fusion.89
  632.0 7.2 fusion.90
  647.2 7.3 copy.55
  654.5 7.3 copy.57
  661.8 3.5 fusion.89
  675.4 7.2 fusion.90
  690.7 7.3 copy.55
  698.0 7.3 copy.57
  705.3 3.5 fusion.89
  718.9 7.2 fusion.90
  734.2 7.3 copy.55
  741.5 7.3 copy.57
  748.8 3.5 fusion.89
  762.4 7.2 fusion.90
  777.6 7.3 copy.55
  784.9 7.3 copy.57
  792.2 3.5 fusion.89
  805.9 7.2 fusion.90
  821.1 7.3 copy.55
  828.4 7.3 copy.57
  849.4 7.2 fusion.90
  858.8 7.2 bitcast_divide_fusion
  (152 shorter events, 166.4 us)
Async XLA Ops:
  12.3 34.3 %copy-start.3 = (bf16[512,2000]{1,0:T(8,128)(2,1)S(1)}, bf16[512,2000]{1,0:T(8,128)(2,1)}, u32[]{:S(2)}) copy-start(bf16[512,2000]{1,0:T(8,128)(2,1)} %reshape.68) | copy-start | bytes 6144004
  68.4 98.4 %copy-start.6 = (s32[64]{0:T(128)S(1)}, s32[64]{0:T(128)}, u32[]{:S(2)}) copy-start(s32[64]{0:T(128)} %param.6) | copy-start | bytes 772
  68.4 98.4 %all-to-all-start = ((bf16[4,128,4,2000]{1,3,2,0:T(8,128)(2,1)}), bf16[4,128,4,2000]{1,3,2,0:T(8,128)(2,1)}, u32[]{:S(2)}, u32[]{:S(2)}) async-start(bf16[4,128,4,2000]{1,3,2,0:T(8,128)(2,1)} %stack.3), calls=%async_computation | async-start | bytes 16384000 | tf_op jit(solution)/shard_map/all_to_all | solution.py:13
  74.2 432.3 %all-reduce.2.cloned.1.call-start = ((), (), s32[]{:S(2)}) async-start(), calls=%async_computation.1 | async-start | bytes 8388608 | tf_op jit(solution)/shard_map/psum | solution.py:65
  184.8 0.7 copy-start.5
  511.1 347.8 %copy-start.4 = (f32[64,128]{1,0:T(8,128)S(1)}, f32[64,128]{1,0:T(8,128)}, u32[]{:S(2)}) copy-start(f32[64,128]{1,0:T(8,128)} %convolution_maximum_fusion) | copy-start | bytes 98308
  531.4 3.5 copy-start.1
  531.4 4.0 copy-start.2
  535.4 3.2 copy-start
  574.9 3.5 copy-start.1
  574.9 4.0 copy-start.2
  578.9 3.2 copy-start
  618.3 3.5 copy-start.1
  618.3 4.0 copy-start.2
  622.4 3.2 copy-start
  661.8 3.5 copy-start.1
  661.8 4.0 copy-start.2
  665.8 3.2 copy-start
  705.3 3.5 copy-start.1
  705.3 4.0 copy-start.2
  709.3 3.2 copy-start
  748.8 3.5 copy-start.1
  748.8 4.0 copy-start.2
  752.8 3.2 copy-start
  792.2 3.5 copy-start.1
  792.2 4.0 copy-start.2
  796.3 3.2 copy-start
  835.7 3.5 copy-start.1
  835.7 4.0 copy-start.2
  839.8 3.2 copy-start
Sparse Core Ops, SparseCore 0:
  184.9 321.5 all-reduce.1
